TPU v7x, 256 devices: a whole 4x4x8 slice. The times are simulated.
256 devices in a mesh: chan: 64 (over z_hi, x, y, core), tm: 4 (over z_lo).
Axes of the slice: x: 4, y: 4, z: 8 (z_hi: 2, z_lo: 4; z = z_hi * 4 + z_lo), core: 2. Of those that a mesh axis runs over, the one named last changes fastest.
Arguments:
- spectra: bfloat16 [64, 8, 2, 6144], P(None, 'tm', None, 'chan'), may hold values from -120 to 120
- bad_channels: int32 [6144], P('chan'), may hold values 0 or 1
- tile_list: int32 [512, 2], P('chan'), may hold values from 0 to 47, as said below
Outputs:
- correlations: float32 [512, 32, 128, 128], P(('chan', 'tm'))
Inputs may be any that keep to these rules, and one draw needn't show every extreme that they name: `tile_list`: each row (a, b) has a <= b; a pair may appear more than once.
All inputs are finite; a program needn't handle non-finite values. No bound on the sum of `bad_channels` on one device may be relied on, other than what follows from the above.
Results may differ from a plain program's by a relative error of at most 0.004.
Values may be sent and summed in bfloat16 or wider, within the bound.
A program may use at most 128 MiB of HBM per device.

v0:
```python
import math
import jax
import jax.numpy as jnp
from jax import lax
from jax.sharding import PartitionSpec as P

HR_DEV = 2
F = 64
LAGS = 32
TILE = 128
EPSILON = 1e-06


def whiten(spectra, bad_channels):
    values = spectra.astype(jnp.float32)
    power = jnp.mean(values * values, axis=(0, 2))
    keep_mask = (1 - bad_channels).astype(jnp.float32)
    white = values * lax.rsqrt(power + EPSILON)[None, :, None, :] * keep_mask[None, None, None, :]
    return white.astype(jnp.bfloat16)


def lag_table(hour_count):
    bin_number = jnp.arange(F, dtype=jnp.float32) + 1.0
    lag_steps = jnp.arange(LAGS, dtype=jnp.float32) - float(LAGS // 2)
    phases = math.pi / F * bin_number[:, None] * lag_steps[None, :]
    norm_scale = 1.0 / math.sqrt(F * hour_count)
    return jnp.stack([jnp.cos(phases) * norm_scale, -jnp.sin(phases) * norm_scale], axis=1)


def take_block(spectra_all, block_index):
    return lax.dynamic_slice_in_dim(spectra_all, block_index * TILE, TILE, axis=3)


def cross_spec(spectra_all, tile_pair):
    left_block = take_block(spectra_all, tile_pair[0])
    right_block = take_block(spectra_all, tile_pair[1])
    bin_total = left_block.shape[0]
    hour_count = left_block.shape[1]
    row_block = left_block.reshape(bin_total, 2 * hour_count, TILE)
    turned = jnp.stack([-right_block[:, :, 1], right_block[:, :, 0]], axis=2)
    col_block = jnp.concatenate([right_block, turned], axis=3).reshape(
        bin_total, 2 * hour_count, 2 * TILE
    )
    return jnp.einsum("fki,fkj->fij", row_block, col_block, preferred_element_type=jnp.float32)


def transform(cross, table):
    parted = cross.reshape(cross.shape[0], TILE, 2, TILE)
    return jnp.einsum("fixj,fxt->tij", parted, table, precision=lax.Precision.HIGHEST)


def tile_lags(spectra_all, table, pairs):
    return jax.vmap(lambda tile_pair: transform(cross_spec(spectra_all, tile_pair), table))(pairs)


def per_device(spectra, bad_channels, tile_list):
    white = whiten(spectra, bad_channels)
    tile_dev = tile_list.shape[0] // lax.axis_size("tm")
    table = lag_table(HR_DEV * lax.axis_size("tm"))
    hours_all = lax.all_gather(white, "tm", axis=1, tiled=True)
    spectra_all = lax.all_gather(hours_all, "chan", axis=3, tiled=True)
    own_pairs = lax.dynamic_slice_in_dim(
        tile_list, lax.axis_index("tm") * tile_dev, tile_dev, axis=0
    )
    return tile_lags(spectra_all, table, own_pairs)


def solution(mesh):
    placed = (P(None, "tm", None, "chan"), P("chan"), P("chan", None))
    return jax.shard_map(
        per_device,
        mesh=mesh,
        in_specs=placed,
        out_specs=P(("chan", "tm"), None, None, None),
        check_vma=False,
    )
```

profile of v0, /device:TPU:1, one launch (start us, length us, event | category | flops | bytes accessed | tf_op | source)
XLA Modules:
  0.0 306.1 jit_solution(9711034003275333782)
XLA Ops:
  6.5 0.0 copy-start
  6.5 0.0 all-gather.2.cloned.1.call-start
  6.5 0.9 fusion.7
  7.4 0.7 subtract_convert_fusion
  8.1 0.9 fusion.9
  9.0 13.7 %all_gather.6 = bf16[64,8,2,96]{3,0,2,1:T(8,128)(2,1)S(1)} all-gather(bf16[64,2,2,96]{3,0,2,1:T(8,128)(2,1)S(1)} %fusion.9), channel_id=1, replica_groups=mesh['chan'=64,'tm'=4] {'tm'}, dimensions={1}, use_global_device_ids=true | all-gather | bytes 245760 | tf_op jit(solution)/shard_map/all_gather | solution.py:60
  22.7 1.1 copy.15
  23.7 0.0 all-gather.2.cloned.1.call-update
  23.8 0.0 copy-done
  23.8 0.1 constant_dynamic-slice_fusion
  23.9 0.1 fusion.12
  24.0 204.5 %all-gather.2.cloned.1.call-done = bf16[64,8,2,6144]{0,1,2,3:T(8,128)(2,1)} async-done(((bf16[64,8,2,96]{0,1,2,3:T(8,128)(2,1)}), bf16[64,8,2,6144]{0,1,2,3:T(8,128)(2,1)}) %all-gather.2.cloned.1.call-update) | async-done | bytes 12582928 | tf_op jit(solution)/shard_map/all_gather | solution.py:61
  228.5 8.9 %gather_fusion.1 = bf16[2,64,8,2,128]{1,2,3,4,0:T(8,128)(2,1)S(1)} fusion(bf16[64,8,2,6144]{0,1,2,3:T(8,128)(2,1)} %all-gather.2.cloned.1.call-done, s32[2]{0:T(128)S(1)} %get-tuple-element.10), kind=kCustom, calls=%fused_computation.1 | custom fusion | bytes 1048608 | tf_op jit(solution)/shard_map/vmap()/gather | solution.py:31
  237.4 0.1 slice_negate_fusion
  237.6 0.5 maximum_maximum_fusion
  238.1 3.1 %copy.17 = bf16[2,64,8,2,256]{4,3,2,1,0:T(2,128)(2,1)S(1)} copy(bf16[2,64,8,2,256]{1,2,3,4,0:T(8,128)(2,1)S(1)} %maximum_maximum_fusion) | data formatting | bytes 2097152 | tf_op jit(solution)/shard_map/vmap()/concatenate | solution.py:41
  241.2 0.4 reshape.116
  241.6 8.9 %gather_fusion = bf16[2,64,8,2,128]{1,2,3,4,0:T(8,128)(2,1)S(1)} fusion(bf16[64,8,2,6144]{0,1,2,3:T(8,128)(2,1)} %all-gather.2.cloned.1.call-done, s32[2]{0:T(128)S(1)} %get-tuple-element.9), kind=kCustom, calls=%fused_computation | custom fusion | bytes 1048608 | tf_op jit(solution)/shard_map/vmap()/gather | solution.py:31
  250.5 0.9 copy.16
  251.4 8.1 %fusion.5 = f32[2,64,128,256]{3,2,1,0:T(8,128)} fusion(bf16[2,64,16,256]{3,2,1,0:T(8,128)(2,1)S(1)} %reshape.116, bf16[2,64,16,128]{3,1,2,0:T(8,128)(2,1)S(1)} %bitcast.18), kind=kOutput, calls=%fused_computation.7 | convolution fusion | flops 134217728 | bytes 18350080 | tf_op jit(solution)/shard_map/vmap(fki,fkj->fij)/dot_general | solution.py:44
  259.5 0.0 copy-start.1
  259.5 20.8 %reshape.117 = f32[2,64,128,2,128]{4,3,2,1,0:T(2,128)} reshape(f32[2,64,128,256]{3,2,1,0:T(8,128)} %fusion.5) | data formatting | bytes 33554432 | tf_op jit(solution)/shard_map/vmap()/reshape | solution.py:48
  280.3 14.5 %fusion.2 = f32[2,32,128,128]{3,1,2,0:T(8,128)S(1)} fusion(f32[2,64,128,2,128]{4,3,2,1,0:T(2,128)} %reshape.117, f32[64,1,32]{0,2,1:T(8,128)S(1)} %get-tuple-element.8, f32[64,1,32]{0,2,1:T(8,128)S(1)} %get-tuple-element.7), kind=kOutput, calls=%fused_computation.4 | convolution fusion | flops 1610616832 | bytes 20987904 | tf_op jit(solution)/shard_map/vmap(fixj,fxt->tij)/dot_general | solution.py:49
  294.8 4.4 %copy.20 = f32[2,32,128,128]{3,2,1,0:T(8,128)} copy(f32[2,32,128,128]{3,1,2,0:T(8,128)S(1)} %fusion.2) | data formatting | bytes 8388608 | tf_op jit(solution)/shard_map/vmap()/transpose | solution.py:53
  299.2 0.0 copy-done.1
  (4 shorter events, 0.0 us)
Async XLA Ops:
  6.5 17.3 %copy-start = (s32[8,2]{0,1:T(2,128)S(1)}, s32[8,2]{0,1:T(2,128)}, u32[]{:S(2)}) copy-start(s32[8,2]{0,1:T(2,128)} %param.5) | copy-start | bytes 196
  6.5 222.0 %all-gather.2.cloned.1.call-start = ((), (), s32[]{:S(2)}) async-start(), calls=%async_computation | async-start | bytes 25559040 | tf_op jit(solution)/shard_map/all_gather | solution.py:61
  259.5 39.7 %copy-start.1 = (s32[8,2]{0,1:T(2,128)S(1)}, s32[8,2]{0,1:T(2,128)}, u32[]{:S(2)}) copy-start(s32[8,2]{0,1:T(2,128)} %param.5) | copy-start | bytes 196
Sparse Core Ops, SparseCore 0:
  23.9 204.5 all-gather.1
where the time goes:
time: 307 us; the launch traced here: 306 us
  waiting for transfers between devices  205 us (67%)
  local copies, waits for them, and re-layouts  48.6 us (16%)
  matrix products  22.6 us (7%)
  blocking collectives  13.7 us (4%)
  between operations  13.5 us (4%)
  other arithmetic  3.19 us (1%)
    all_gather x1, waiting for transfers between devices, per_device(): spectra_all = lax.all_gather(hours_all, 'chan', axis=3, tiled=True)  204 us
    reshape x1, local copies, waits for them, and re-layouts, transform(): parted = cross.reshape(cross.shape[0], TILE, 2, TILE)  20.8 us
    gather x3, local copies, waits for them, and re-layouts, take_block(): lax.dynamic_slice_in_dim(spectra_all, block_index * TILE, TILE, axis=3)  18.7 us
    dot_general x1, matrix products, transform(): jnp.einsum('fixj,fxt->tij', parted, table, precision=lax.Precision.HIGHEST)  14.5 us
    all_gather x1, blocking collectives, per_device(): hours_all = lax.all_gather(white, 'tm', axis=1, tiled=True)  13.7 us
    dot_general x1, matrix products, cross_spec(): jnp.einsum('fki,fkj->fij', row_block, col_block, preferred_element_type=j...  8.11 us
  transfers between devices with their start and end apart: 1, of which 1 were waited for; matrix products, arithmetic and copies ran while one was open for 0% of the time, Pallas kernels for 0%

commit v1 on v0

--- a/solution.py
+++ b/solution.py
@@ -58,7 +58,9 @@
     tile_dev = tile_list.shape[0] // lax.axis_size("tm")
     table = lag_table(HR_DEV * lax.axis_size("tm"))
     hours_all = lax.all_gather(white, "tm", axis=1, tiled=True)
-    spectra_all = lax.all_gather(hours_all, "chan", axis=3, tiled=True)
+    spectra_all = jnp.concatenate(
+        lax.all_to_all(jnp.stack([hours_all] * lax.axis_size("chan")), "chan", 0, 0), axis=3
+    )
     own_pairs = lax.dynamic_slice_in_dim(
         tile_list, lax.axis_index("tm") * tile_dev, tile_dev, axis=0
     )

time: 307 us -> 536 us (1.75)
  waiting for transfers between devices: 205 us -> 385 us
  local copies, waits for them, and re-layouts: 48.6 us -> 91.3 us
  starting transfers between devices: 0.01 us -> 14.4 us
  between operations: 13.5 us -> 0.11 us
    all_to_all x0 -> x1, waiting for transfers between devices: none -> 385 us  [per_device(): lax.all_to_all(jnp.stack([hours_all] * lax.axis_size('chan')), 'chan', 0, 0)]
    all_gather x1 -> x0, waiting for transfers between devices: 204 us -> none  [per_device(): spectra_all = lax.all_gather(hours_all, 'chan', axis=3, tiled=True)]
    reshape x0 -> x1, local copies, waits for them, and re-layouts: none -> 37.4 us  [per_device(): jnp.concatenate(lax.all_to_all(jnp.stack([hours_all] * lax.axis_size('cha...]
    all_to_all x0 -> x1, starting transfers between devices: none -> 14.4 us  [per_device(): lax.all_to_all(jnp.stack([hours_all] * lax.axis_size('chan')), 'chan', 0, 0)]
    another operation x0 -> x1, local copies, waits for them, and re-layouts: none -> 6.28 us  [per_device(): jnp.stack([hours_all] * lax.axis_size('chan'))]
where the time goes in v1:
time: 536 us; the launch traced here: 530 us
  waiting for transfers between devices  385 us (72%)
  local copies, waits for them, and re-layouts  91.3 us (17%)
  matrix products  22.7 us (4%)
  starting transfers between devices  14.4 us (3%)
  blocking collectives  13.3 us (2%)
    all_to_all x1, waiting for transfers between devices, per_device(): lax.all_to_all(jnp.stack([hours_all] * lax.axis_size('chan')), 'chan', 0, 0)  385 us
    reshape x1, local copies, waits for them, and re-layouts, per_device(): jnp.concatenate(lax.all_to_all(jnp.stack([hours_all] * lax.axis_size('cha...  37.4 us
    reshape x1, local copies, waits for them, and re-layouts, transform(): parted = cross.reshape(cross.shape[0], TILE, 2, TILE)  20.8 us
    gather x3, local copies, waits for them, and re-layouts, take_block(): lax.dynamic_slice_in_dim(spectra_all, block_index * TILE, TILE, axis=3)  18.7 us
    dot_general x1, matrix products, transform(): jnp.einsum('fixj,fxt->tij', parted, table, precision=lax.Precision.HIGHEST)  14.6 us
    all_to_all x1, starting transfers between devices, per_device(): lax.all_to_all(jnp.stack([hours_all] * lax.axis_size('chan')), 'chan', 0, 0)  14.4 us
    all_gather x1, blocking collectives, per_device(): hours_all = lax.all_gather(white, 'tm', axis=1, tiled=True)  13.3 us
  transfers between devices with their start and end apart: 1, of which 1 were waited for; matrix products, arithmetic and copies ran while one was open for 0% of the time, Pallas kernels for 0%

profile of v1, /device:TPU:1, one launch (start us, length us, event | category | flops | bytes accessed | tf_op | source)
XLA Modules:
  0.0 530.3 jit_solution(6958903352883062216)
XLA Ops:
  0.0 0.0 copy-start
  0.0 0.7 subtract_convert_fusion
  0.7 1.0 fusion.7
  1.6 0.9 fusion.9
  2.6 13.3 %all_gather.3 = bf16[64,8,2,96]{3,2,1,0:T(2,128)(2,1)S(1)} all-gather(bf16[64,2,2,96]{3,2,1,0:T(2,128)(2,1)S(1)} %fusion.9), channel_id=1, replica_groups=mesh['chan'=64,'tm'=4] {'tm'}, dimensions={1}, use_global_device_ids=true | all-gather | bytes 245760 | tf_op jit(solution)/shard_map/all_gather | solution.py:60
  15.9 6.3 %stack.7 = bf16[64,64,8,2,96]{4,2,3,1,0:T(8,128)(2,1)} broadcast(bf16[64,8,2,96]{3,1,2,0:T(8,128)(2,1)S(1)} %copy.14), dimensions={1,2,3,4} | broadcast | bytes 12779520 | tf_op jit(solution)/shard_map/stack | solution.py:62
  22.2 14.4 %all-to-all-start = ((bf16[64,64,8,2,96]{4,2,3,1,0:T(8,128)(2,1)}), bf16[64,64,8,2,96]{4,2,3,1,0:T(8,128)(2,1)}, u32[]{:S(2)}, u32[]{:S(2)}) async-start(bf16[64,64,8,2,96]{4,2,3,1,0:T(8,128)(2,1)} %stack.7), calls=%async_computation | async-start | bytes 33554432 | tf_op jit(solution)/shard_map/all_to_all | solution.py:62
  36.7 0.0 copy-done
  36.7 0.1 constant_dynamic-slice_fusion
  36.8 0.1 fusion.12
  36.9 385.1 %all-to-all-done = bf16[64,64,8,2,96]{4,2,3,1,0:T(8,128)(2,1)} async-done(((bf16[64,64,8,2,96]{4,2,3,1,0:T(8,128)(2,1)}), bf16[64,64,8,2,96]{4,2,3,1,0:T(8,128)(2,1)}, u32[]{:S(2)}, u32[]{:S(2)}) %all-to-all-start) | async-done | bytes 12582944 | tf_op jit(solution)/shard_map/all_to_all | solution.py:62
  422.0 37.4 %copy.15 = bf16[64,8,2,64,96]{0,1,2,4,3:T(8,128)(2,1)} copy(bf16[64,8,2,64,96]{4,1,2,0,3:T(8,128)(2,1)} %bitcast.2) | data formatting | bytes 25165824 | tf_op jit(solution)/shard_map/reshape | solution.py:61
  459.4 8.9 %gather_fusion.1 = bf16[2,64,8,2,128]{1,2,3,4,0:T(8,128)(2,1)S(1)} fusion(bf16[64,8,2,6144]{0,1,2,3:T(8,128)(2,1)} %bitcast.20, s32[2]{0:T(128)S(1)} %get-tuple-element.10), kind=kCustom, calls=%fused_computation.1 | custom fusion | bytes 1048608 | tf_op jit(solution)/shard_map/vmap()/gather | solution.py:31
  468.3 0.1 slice_negate_fusion
  468.5 0.5 maximum_maximum_fusion
  469.0 3.1 copy.17
  472.1 0.4 reshape.126
  472.5 8.9 %gather_fusion = bf16[2,64,8,2,128]{1,2,3,4,0:T(8,128)(2,1)S(1)} fusion(bf16[64,8,2,6144]{0,1,2,3:T(8,128)(2,1)} %bitcast.21, s32[2]{0:T(128)S(1)} %get-tuple-element.9), kind=kCustom, calls=%fused_computation | custom fusion | bytes 1048608 | tf_op jit(solution)/shard_map/vmap()/gather | solution.py:31
  481.4 0.9 copy.16
  482.3 8.1 %fusion.5 = f32[2,64,128,256]{3,2,1,0:T(8,128)} fusion(bf16[2,64,16,256]{3,2,1,0:T(8,128)(2,1)S(1)} %reshape.126, bf16[2,64,16,128]{3,1,2,0:T(8,128)(2,1)S(1)} %bitcast.22), kind=kOutput, calls=%fused_computation.7 | convolution fusion | flops 134217728 | bytes 18350080 | tf_op jit(solution)/shard_map/vmap(fki,fkj->fij)/dot_general | solution.py:44
  490.4 0.0 copy-start.1
  490.4 20.8 %reshape.127 = f32[2,64,128,2,128]{4,3,2,1,0:T(2,128)} reshape(f32[2,64,128,256]{3,2,1,0:T(8,128)} %fusion.5) | data formatting | bytes 33554432 | tf_op jit(solution)/shard_map/vmap()/reshape | solution.py:48
  511.2 14.6 %fusion.2 = f32[2,32,128,128]{3,1,2,0:T(8,128)S(1)} fusion(f32[2,64,128,2,128]{4,3,2,1,0:T(2,128)} %reshape.127, f32[64,1,32]{0,2,1:T(8,128)S(1)} %get-tuple-element.8, f32[64,1,32]{0,2,1:T(8,128)S(1)} %get-tuple-element.7), kind=kOutput, calls=%fused_computation.4 | convolution fusion | flops 1610616832 | bytes 20987904 | tf_op jit(solution)/shard_map/vmap(fixj,fxt->tij)/dot_general | solution.py:49
  525.9 4.4 copy.20
  530.3 0.0 copy-done.1
  (5 shorter events, 0.1 us)
Async XLA Ops:
  0.0 36.7 %copy-start = (s32[8,2]{0,1:T(2,128)S(1)}, s32[8,2]{0,1:T(2,128)}, u32[]{:S(2)}) copy-start(s32[8,2]{0,1:T(2,128)} %param.5) | copy-start | bytes 196
  22.2 399.8 %all-to-all-start = ((bf16[64,64,8,2,96]{4,2,3,1,0:T(8,128)(2,1)}), bf16[64,64,8,2,96]{4,2,3,1,0:T(8,128)(2,1)}, u32[]{:S(2)}, u32[]{:S(2)}) async-start(bf16[64,64,8,2,96]{4,2,3,1,0:T(8,128)(2,1)} %stack.7), calls=%async_computation | async-start | bytes 33554432 | tf_op jit(solution)/shard_map/all_to_all | solution.py:62
  490.4 39.9 %copy-start.1 = (s32[8,2]{0,1:T(2,128)S(1)}, s32[8,2]{0,1:T(2,128)}, u32[]{:S(2)}) copy-start(s32[8,2]{0,1:T(2,128)} %param.5) | copy-start | bytes 196
